TPU v7x, 32 devices: a whole 2x2x4 slice. The times are simulated.
32 devices in a mesh: span: 8 (over y, x, core), head: 4 (over z).
Axes of the slice: x: 2, y: 2, z: 4, core: 2. Of those that a mesh axis runs over, the one named last changes fastest.
Arguments:
- neighbour_query: bfloat16 [8192, 4096], P('span', 'head'), may hold values from -12 to 12
- neighbour_key: bfloat16 [8192, 4096], P('span', 'head'), may hold values from -6 to 6
- neighbour_value: bfloat16 [8192, 4096], P('span', 'head'), may hold values from -12.2 to 12.2
- segment_key: bfloat16 [2048, 4096], P('span', 'head'), may hold values from -30 to 30
- segment_value: bfloat16 [2048, 4096], P('span', 'head'), may hold values from -6 to 6
- decoder_query: bfloat16 [2048, 4096], P('span', 'head'), may hold values from -24 to 24
- sources: int32 [32, 2], P('span'), may hold values from 0 to 31, as said below
Outputs:
- blended: bfloat16 [2048, 4096], P('span', 'head')
Inputs may be any that keep to these rules, and one draw needn't show every extreme that they name: `sources`: the segments of index o of span are o * 4 to (o + 1) * 4 - 1. Among the 8 entries of the segments of one index of span, at most 2 name segments of one index of span, and in every such block some index is named exactly 2 times.
All inputs are finite; a program needn't handle non-finite values.
Results may differ from a plain program's by a relative error of at most 0.035.
Values may be sent and summed in bfloat16 or wider, within the bound.
A program may use at most 192 MiB of HBM per device.

v0:
```python
import jax
import jax.numpy as jnp
from jax import lax
from jax.sharding import PartitionSpec as P

HEAD_DIM = 128
SEG_LEN = 64
NBR_LEN = 128
NEIGHBOURS = 2
SEG_DEV = 4


epsilon = 1e-06


def from_behind(x, axis, by):
    count = lax.axis_size(axis)
    pairs = [(i, i + by) for i in range(count) if 0 <= i + by < count]
    return lax.ppermute(x, axis, pairs)


def attend(query_rows, key_rows, value_rows):
    groups, length, columns = query_rows.shape
    head_count = columns // HEAD_DIM
    query_heads = query_rows.reshape(groups, length, head_count, HEAD_DIM)
    key_heads = key_rows.reshape(groups, key_rows.shape[1], head_count, HEAD_DIM)
    value_heads = value_rows.reshape(groups, value_rows.shape[1], head_count, HEAD_DIM)
    logit_scores = jnp.einsum(
        "bqhd,bkhd->bhqk", query_heads, key_heads, preferred_element_type=jnp.float32
    ) * HEAD_DIM ** (-0.5)
    logit_scores = logit_scores - jnp.max(logit_scores, axis=-1, keepdims=True)
    weights = jnp.exp(logit_scores)
    weights = (weights / jnp.sum(weights, axis=-1, keepdims=True)).astype(jnp.bfloat16)
    output = jnp.einsum("bhqk,bkhd->bqhd", weights, value_heads, preferred_element_type=jnp.float32)
    return output.reshape(groups, length, columns)


def squares(rows):
    wide = rows.astype(jnp.float32)
    return jnp.sum(wide * wide, axis=-1)


def normalize(rows, totals, full_width):
    scale = lax.rsqrt(totals / full_width + epsilon)
    return (rows.astype(jnp.float32) * scale[:, None]).astype(jnp.bfloat16)


def body(
    neighbour_query,
    neighbour_key,
    neighbour_value,
    segment_key,
    segment_value,
    decoder_query,
    sources,
):
    columns = neighbour_query.shape[1]
    full_width = columns * lax.axis_size("head")
    devices = lax.axis_size("span")
    per_device = SEG_DEV * NEIGHBOURS
    capacity = max(2, 2 * per_device // devices)
    panel_rows = NEIGHBOURS * NBR_LEN
    self_out = attend(
        neighbour_query.reshape(per_device, NBR_LEN, columns),
        neighbour_key.reshape(per_device, NBR_LEN, columns),
        neighbour_value.reshape(per_device, NBR_LEN, columns),
    ).astype(jnp.bfloat16)
    flat_self = self_out.reshape(per_device * NBR_LEN, columns)
    totals = lax.psum(squares(flat_self), "head")
    cross_query = normalize(flat_self, totals, full_width).reshape(per_device, NBR_LEN, columns)
    listed = sources.reshape(per_device)
    owners = listed // SEG_DEV
    within = listed % SEG_DEV
    position = jnp.arange(per_device)
    earlier = (owners[:, None] == owners[None, :]) & (position[:, None] > position[None, :])
    ranked = jnp.sum(earlier.astype(jnp.int32), axis=1)
    slots = owners * capacity + ranked
    picked = (slots[:, None] == jnp.arange(devices * capacity)[None, :]).astype(jnp.int32)
    request = jnp.sum(picked * (within + 1)[:, None], axis=0).reshape(devices, capacity)
    asked = lax.all_to_all(request, "span", split_axis=0, concat_axis=0, tiled=True)
    wanted = jnp.maximum(asked - 1, 0).reshape(devices * capacity)
    own_keys = segment_key.reshape(SEG_DEV, SEG_LEN, columns)[wanted]
    own_values = segment_value.reshape(SEG_DEV, SEG_LEN, columns)[wanted]
    got_keys, got_values = (
        lax.all_to_all(
            own_keys.reshape(devices, capacity, SEG_LEN, columns),
            "span",
            split_axis=0,
            concat_axis=0,
            tiled=True,
        ),
        lax.all_to_all(
            own_values.reshape(devices, capacity, SEG_LEN, columns),
            "span",
            split_axis=0,
            concat_axis=0,
            tiled=True,
        ),
    )
    source_keys = got_keys.reshape(devices * capacity, SEG_LEN, columns)[slots]
    source_values = got_values.reshape(devices * capacity, SEG_LEN, columns)[slots]
    crossed = attend(cross_query, source_keys, source_values).astype(jnp.bfloat16)
    encoded = (self_out.astype(jnp.float32) + crossed.astype(jnp.float32)).astype(jnp.bfloat16)
    encoded = encoded.reshape(per_device * NBR_LEN, columns)
    key_totals = lax.psum(squares(encoded), "head")
    keys_all = normalize(encoded, key_totals, full_width)
    before_keys, before_values = from_behind(
        (keys_all[-panel_rows:], encoded[-panel_rows:]), "span", 1
    )
    used_keys = jnp.concatenate([before_keys, keys_all[:-panel_rows]], axis=0)
    used_values = jnp.concatenate([before_values, encoded[:-panel_rows]], axis=0)
    blended = attend(
        decoder_query.reshape(SEG_DEV, SEG_LEN, columns),
        used_keys.reshape(SEG_DEV, panel_rows, columns),
        used_values.reshape(SEG_DEV, panel_rows, columns),
    ).astype(jnp.bfloat16)
    return blended.reshape(SEG_DEV * SEG_LEN, columns)


def solution(mesh):
    placed = (
        P("span", "head"),
        P("span", "head"),
        P("span", "head"),
        P("span", "head"),
        P("span", "head"),
        P("span", "head"),
        P("span", None),
    )
    return jax.shard_map(
        body, mesh=mesh, in_specs=placed, out_specs=P("span", "head"), check_vma=False
    )
```

profile of v0, /device:TPU:0, one launch (start us, length us, event | category | flops | bytes accessed | tf_op | source)
XLA Modules:
  0.0 126.3 jit_solution(12153524779361700887)
XLA Ops:
  1.3 9.7 %all_to_all.19 = s32[8,1,2]{2,1,0:T(1,128)S(1)} all-to-all(s32[8,1,2]{2,1,0:T(1,128)S(1)} %bitcast.126), channel_id=1, replica_groups=mesh['span'=8,'head'=4] {'span'}, dimensions={0} | all-to-all | bytes 128 | tf_op jit(solution)/shard_map/all_to_all | solution.py:80
  11.1 2.0 %gather_fusion.2 = bf16[16,64,1024]{2,1,0:T(8,128)(2,1)} fusion(bf16[4,64,1024]{2,1,0:T(8,128)(2,1)S(1)} %bitcast.108, s32[1024]{0:T(1024)S(1)} %pad_clamp_fusion.1), kind=kCustom, calls=%fused_computation.2 | custom fusion | bytes 4194368 | tf_op jit(solution)/shard_map/gather | solution.py:82
  13.1 3.6 %all-to-all-start.2 = ((bf16[8,2,64,1024]{3,2,1,0:T(8,128)(2,1)}), bf16[8,2,64,1024]{3,2,1,0:T(8,128)(2,1)S(1)}, u32[]{:S(2)}, u32[]{:S(2)}) async-start(bf16[8,2,64,1024]{3,2,1,0:T(8,128)(2,1)} %bitcast.10), calls=%async_computation.2 | async-start | bytes 4194304 | tf_op jit(solution)/shard_map/all_to_all | solution.py:85
  16.8 2.4 %copy.72 = bf16[128,8,8,128]{3,2,1,0:T(8,128)(2,1)S(1)} copy(bf16[128,8,8,128]{3,1,2,0:T(8,128)(2,1)} %bitcast.118) | data formatting | bytes 4194304
  20.8 1.9 %copy.70 = bf16[128,8,8,128]{3,2,1,0:T(8,128)(2,1)} copy(bf16[128,8,8,128]{3,1,2,0:T(8,128)(2,1)S(1)} %bitcast.120) | data formatting | bytes 4194304
  24.3 3.0 %fusion.68 = (f32[8,8,128]{2,1,0:T(8,128)S(1)}, f32[8,8,128,128]{2,3,1,0:T(8,128)}) fusion(f32[8,8,128,128]{2,3,1,0:T(8,128)S(1)} %fusion.20), kind=kOutput, calls=%fused_computation.91 | output fusion | flops 4194431 | bytes 8421376 | tf_op jit(solution)/shard_map/sub | solution.py:31
  27.2 2.1 %gather_fusion = bf16[16,64,1024]{2,1,0:T(8,128)(2,1)} fusion(bf16[4,64,1024]{2,1,0:T(8,128)(2,1)S(1)} %bitcast.111, s32[1024]{0:T(1024)S(1)} %pad_clamp_fusion.1), kind=kCustom, calls=%fused_computation | custom fusion | bytes 4194368 | tf_op jit(solution)/shard_map/gather | solution.py:83
  29.3 13.9 %all-to-all-done.2 = bf16[8,2,64,1024]{3,2,1,0:T(8,128)(2,1)S(1)} async-done(((bf16[8,2,64,1024]{3,2,1,0:T(8,128)(2,1)}), bf16[8,2,64,1024]{3,2,1,0:T(8,128)(2,1)S(1)}, u32[]{:S(2)}, u32[]{:S(2)}) %all-to-all-start.2) | async-done | bytes 2097184 | tf_op jit(solution)/shard_map/all_to_all | solution.py:85
  43.3 4.3 %all-to-all-start.1 = ((bf16[8,2,64,1024]{3,2,1,0:T(8,128)(2,1)}), bf16[8,2,64,1024]{3,2,1,0:T(8,128)(2,1)}, u32[]{:S(2)}, u32[]{:S(2)}) async-start(bf16[8,2,64,1024]{3,2,1,0:T(8,128)(2,1)} %bitcast.3), calls=%async_computation.1 | async-start | bytes 4194304 | tf_op jit(solution)/shard_map/all_to_all | solution.py:92
  47.6 5.3 %fusion.5 = (f32[8,128]{1,0:T(8,128)S(1)}, bf16[8,8,128,128]{2,3,1,0:T(8,128)(2,1)}) fusion(f32[8,8,128,128]{2,3,1,0:T(8,128)} %get-tuple-element.8, f32[8,8,128]{2,1,0:T(8,128)S(1)} %get-tuple-element.7, bf16[8,128,8,128]{3,2,1,0:T(8,128)(2,1)} %bitcast.121), kind=kOutput, calls=%fused_computation.13 | convolution fusion | flops 274725888 | bytes 8425472 | tf_op jit(solution)/shard_map/bhqk,bkhd->bqhd/dot_general | solution.py:34
  52.9 11.9 %psum.14 = f32[1024]{0:T(1024)S(1)} all-reduce(f32[1024]{0:T(1024)S(1)} %bitcast.128), channel_id=1, replica_groups=mesh['span'=8,'head'=4] {'head'}, use_global_device_ids=true, to_apply=%region_5.6 | all-reduce | flops 1024 | bytes 8192 | tf_op jit(solution)/shard_map/psum | solution.py:69
  64.9 1.6 %gather_fusion.3 = bf16[8,64,1024]{2,1,0:T(8,128)(2,1)} fusion(bf16[16,64,1024]{2,1,0:T(8,128)(2,1)S(1)} %bitcast.116, s32[1024]{0:T(1024)S(1)} %pad_clamp_fusion), kind=kCustom, calls=%fused_computation.3 | custom fusion | bytes 2097184 | tf_op jit(solution)/shard_map/gather | solution.py:100
  66.5 2.6 %fusion.11 = f32[8,8,128,64]{2,3,1,0:T(8,128)S(1)} fusion(bf16[8,8,128,128]{2,3,1,0:T(8,128)(2,1)} %get-tuple-element.10, f32[8,128]{1,0:T(8,128)S(1)} %rsqrt_bitcast_fusion, bf16[8,64,1024]{2,1,0:T(8,128)(2,1)} %gather_fusion.3), kind=kOutput, calls=%fused_computation.21 | convolution fusion | flops 137363456 | bytes 5246976 | tf_op jit(solution)/shard_map/bqhd,bkhd->bhqk/dot_general | solution.py:28
  71.0 3.2 %all-to-all-done.1 = bf16[8,2,64,1024]{3,2,1,0:T(8,128)(2,1)} async-done(((bf16[8,2,64,1024]{3,2,1,0:T(8,128)(2,1)}), bf16[8,2,64,1024]{3,2,1,0:T(8,128)(2,1)}, u32[]{:S(2)}, u32[]{:S(2)}) %all-to-all-start.1) | async-done | bytes 2097184 | tf_op jit(solution)/shard_map/all_to_all | solution.py:92
  74.2 3.2 %gather_fusion.1 = bf16[8,64,1024]{2,1,0:T(8,128)(2,1)} fusion(bf16[16,64,1024]{2,1,0:T(8,128)(2,1)} %bitcast.4, s32[1024]{0:T(1024)S(1)} %pad_clamp_fusion), kind=kCustom, calls=%fused_computation.1 | custom fusion | bytes 2097184 | tf_op jit(solution)/shard_map/gather | solution.py:101
  77.4 4.1 %multiply_reduce_fusion = (f32[8,128]{1,0:T(8,128)S(1)}, bf16[8,128,8,128]{1,3,2,0:T(8,128)(2,1)S(1)}) fusion(f32[8,8,128]{2,1,0:T(8,128)S(1)} %fusion.69, f32[8,8,128,64]{2,3,1,0:T(8,128)} %copy-done.7, bf16[8,8,128,128]{2,3,1,0:T(8,128)(2,1)} %get-tuple-element.10, bf16[8,64,1024]{2,1,0:T(8,128)(2,1)} %gather_fusion.1), kind=kOutput, calls=%fused_computation.15 | convolution fusion | flops 144710720 | bytes 7376896 | tf_op jit(solution)/shard_map/bhqk,bkhd->bqhd/dot_general | solution.py:34
  81.6 3.1 %copy.61 = f32[8,128,8,128]{3,2,1,0:T(8,128)} copy(bf16[8,128,8,128]{1,3,2,0:T(8,128)(2,1)S(1)} %get-tuple-element.12) | data formatting | bytes 6291456 | tf_op jit(solution)/shard_map/convert_element_type | solution.py:45
  85.9 2.1 %collective-permute-start = (bf16[256,1024]{1,0:T(8,128)(2,1)}, bf16[256,1024]{1,0:T(8,128)(2,1)}, u32[]{:S(2)}, u32[]{:S(2)}) collective-permute-start(bf16[256,1024]{1,0:T(8,128)(2,1)} %bitcast.107), channel_id=1, source_target_pairs={{0,4},{4,8},{8,12},{12,16},{16,20},{20,24},{24,28},{1,5},{5,9},{9,... | collective-permute-start | bytes 1572872 | tf_op jit(solution)/shard_map/ppermute | solution.py:19
  88.0 11.9 %psum.15 = f32[1024]{0:T(1024)S(1)} all-reduce(f32[1024]{0:T(1024)S(1)} %bitcast.127), channel_id=1, replica_groups=mesh['span'=8,'head'=4] {'head'}, use_global_device_ids=true, to_apply=%region_9.10 | all-reduce | flops 1024 | bytes 8192 | tf_op jit(solution)/shard_map/psum | solution.py:105
  99.9 3.0 %fusion.3 = bf16[1024,1024]{1,0:T(8,128)(2,1)S(1)} fusion(f32[128,8,8,128]{3,2,1,0:T(8,128)} %bitcast.109, f32[1024]{0:T(1024)S(1)} %add_rsqrt_fusion), kind=kLoop, calls=%fused_computation.8 | loop fusion | flops 2097152 | bytes 6295552 | tf_op jit(solution)/shard_map/convert_element_type | solution.py:45
  103.0 2.1 %collective-permute-start.1 = (bf16[256,1024]{1,0:T(8,128)(2,1)S(1)}, bf16[256,1024]{1,0:T(8,128)(2,1)}, u32[]{:S(2)}, u32[]{:S(2)}) collective-permute-start(bf16[256,1024]{1,0:T(8,128)(2,1)S(1)} %slice.34), channel_id=1, source_target_pairs={{0,4},{4,8},{8,12},{12,16},{16,20},{20,24},{24,28},{1,5},{5,9},{9,... | collective-permute-start | bytes 1572872 | tf_op jit(solution)/shard_map/ppermute | solution.py:19
  107.8 1.8 %copy.60 = bf16[6,128,8,128]{3,2,1,0:T(8,128)(2,1)} copy(bf16[6,128,8,128]{1,3,2,0:T(8,128)(2,1)S(1)} %copy-done.4) | data formatting | bytes 3145728 | tf_op jit(solution)/shard_map/slice | solution.py:111
  109.6 1.8 %copy.114 = bf16[96,8,8,128]{3,1,2,0:T(8,128)(2,1)S(1)} copy(bf16[96,8,8,128]{3,2,1,0:T(8,128)(2,1)} %bitcast.114) | data formatting | bytes 3145728
  119.1 5.9 %fusion.36 = bf16[4,64,8,128]{3,1,2,0:T(8,128)(2,1)S(1)} fusion(bf16[4,256,8,128]{3,2,1,0:T(8,128)(2,1)S(1)} %bitcast.122, f32[4,8,64]{2,1,0:T(8,128)S(1)} %fusion.72, f32[4,8,256,64]{2,3,1,0:T(8,128)} %copy-done.8), kind=kOutput, calls=%fused_computation.48 | convolution fusion | flops 137103616 | bytes 4726784 | tf_op jit(solution)/shard_map/bhqk,bkhd->bqhd/dot_general | solution.py:34
  (56 shorter events, 19.4 us)
Async XLA Ops:
  0.0 11.1 %copy-start = (bf16[256,1024]{1,0:T(8,128)(2,1)S(1)}, bf16[256,1024]{1,0:T(8,128)(2,1)}, u32[]{:S(2)}) copy-start(bf16[256,1024]{1,0:T(8,128)(2,1)} %param.10) | copy-start | bytes 1572868
  13.1 30.2 %all-to-all-start.2 = ((bf16[8,2,64,1024]{3,2,1,0:T(8,128)(2,1)}), bf16[8,2,64,1024]{3,2,1,0:T(8,128)(2,1)S(1)}, u32[]{:S(2)}, u32[]{:S(2)}) async-start(bf16[8,2,64,1024]{3,2,1,0:T(8,128)(2,1)} %bitcast.10), calls=%async_computation.2 | async-start | bytes 4194304 | tf_op jit(solution)/shard_map/all_to_all | solution.py:85
  16.8 2.4 %copy-start.5 = (bf16[1024,1024]{1,0:T(8,128)(2,1)S(1)}, bf16[1024,1024]{1,0:T(8,128)(2,1)}, u32[]{:S(2)}) copy-start(bf16[1024,1024]{1,0:T(8,128)(2,1)} %param.7) | copy-start | bytes 6291460
  19.2 1.6 %copy-start.6 = (bf16[1024,1024]{1,0:T(8,128)(2,1)S(1)}, bf16[1024,1024]{1,0:T(8,128)(2,1)}, u32[]{:S(2)}) copy-start(bf16[1024,1024]{1,0:T(8,128)(2,1)} %param.9) | copy-start | bytes 6291460
  24.3 3.0 %copy-start.3 = (bf16[256,1024]{1,0:T(8,128)(2,1)S(1)}, bf16[256,1024]{1,0:T(8,128)(2,1)}, u32[]{:S(2)}) copy-start(bf16[256,1024]{1,0:T(8,128)(2,1)} %param.11) | copy-start | bytes 1572868
  43.3 31.0 %all-to-all-start.1 = ((bf16[8,2,64,1024]{3,2,1,0:T(8,128)(2,1)}), bf16[8,2,64,1024]{3,2,1,0:T(8,128)(2,1)}, u32[]{:S(2)}, u32[]{:S(2)}) async-start(bf16[8,2,64,1024]{3,2,1,0:T(8,128)(2,1)} %bitcast.3), calls=%async_computation.1 | async-start | bytes 4194304 | tf_op jit(solution)/shard_map/all_to_all | solution.py:92
  69.1 1.4 %copy-start.7 = (f32[8,8,128,64]{2,3,1,0:T(8,128)}, f32[8,8,128,64]{2,3,1,0:T(8,128)S(1)}, u32[]{:S(2)}) copy-start(f32[8,8,128,64]{2,3,1,0:T(8,128)S(1)} %fusion.11) | copy-start | bytes 6291460
  85.9 25.6 %collective-permute-start = (bf16[256,1024]{1,0:T(8,128)(2,1)}, bf16[256,1024]{1,0:T(8,128)(2,1)}, u32[]{:S(2)}, u32[]{:S(2)}) collective-permute-start(bf16[256,1024]{1,0:T(8,128)(2,1)} %bitcast.107), channel_id=1, source_target_pairs={{0,4},{4,8},{8,12},{12,16},{16,20},{20,24},{24,28},{1,5},{5,9},{9,... | collective-permute-start | bytes 1572872 | tf_op jit(solution)/shard_map/ppermute | solution.py:19
  99.9 5.2 %copy-start.9 = (bf16[256,1024]{1,0:T(8,128)(2,1)S(1)}, bf16[256,1024]{1,0:T(8,128)(2,1)}, u32[]{:S(2)}) copy-start(bf16[256,1024]{1,0:T(8,128)(2,1)} %param.12) | copy-start | bytes 1572868
  102.9 3.5 %copy-start.2 = (bf16[1024,1024]{1,0:T(8,128)(2,1)}, bf16[1024,1024]{1,0:T(8,128)(2,1)S(1)}, u32[]{:S(2)}) copy-start(bf16[1024,1024]{1,0:T(8,128)(2,1)S(1)} %fusion.3) | copy-start | bytes 6291460
  103.0 10.4 %collective-permute-start.1 = (bf16[256,1024]{1,0:T(8,128)(2,1)S(1)}, bf16[256,1024]{1,0:T(8,128)(2,1)}, u32[]{:S(2)}, u32[]{:S(2)}) collective-permute-start(bf16[256,1024]{1,0:T(8,128)(2,1)S(1)} %slice.34), channel_id=1, source_target_pairs={{0,4},{4,8},{8,12},{12,16},{16,20},{20,24},{24,28},{1,5},{5,9},{9,... | collective-permute-start | bytes 1572872 | tf_op jit(solution)/shard_map/ppermute | solution.py:19
  106.4 1.4 %copy-start.4 = (bf16[6,128,8,128]{1,3,2,0:T(8,128)(2,1)S(1)}, bf16[6,128,8,128]{1,3,2,0:T(8,128)(2,1)}, u32[]{:S(2)}) copy-start(bf16[6,128,8,128]{1,3,2,0:T(8,128)(2,1)} %slice.37) | copy-start | bytes 4718596
  112.7 1.4 %slice-start = ((bf16[1024,1024]{1,0:T(8,128)(2,1)}), bf16[768,1024]{1,0:T(8,128)(2,1)S(1)}, s32[]{:S(2)}) async-start(bf16[1024,1024]{1,0:T(8,128)(2,1)} %copy-done.2), calls=%async_computation.3 | async-start | bytes 3145728 | tf_op jit(solution)/shard_map/slice | solution.py:110
  116.9 1.4 %copy-start.8 = (f32[4,8,256,64]{2,3,1,0:T(8,128)}, f32[4,8,256,64]{2,3,1,0:T(8,128)S(1)}, u32[]{:S(2)}) copy-start(f32[4,8,256,64]{2,3,1,0:T(8,128)S(1)} %fusion.17) | copy-start | bytes 6291460
  119.1 7.2 %copy-start.1 = (bf16[256,1024]{1,0:T(8,128)(2,1)S(1)}, bf16[256,1024]{1,0:T(8,128)(2,1)}, u32[]{:S(2)}) copy-start(bf16[256,1024]{1,0:T(8,128)(2,1)} %param.10) | copy-start | bytes 1572868
where the time goes:
time: 127 us; the launch traced here: 126 us
  blocking collectives  33.5 us (26%)
  local copies, waits for them, and re-layouts  32.6 us (26%)
  matrix products  20.4 us (16%)
  waiting for transfers between devices  17.1 us (13%)
  starting transfers between devices  12.1 us (10%)
  other arithmetic  10.2 us (8%)
    unnamed x30, local copies, waits for them, and re-layouts  15.8 us
    dot_general x3, matrix products, attend(): jnp.einsum('bhqk,bkhd->bqhd', weights, value_heads, preferred_element_typ...  15.4 us
    all_to_all x1, waiting for transfers between devices, body(): lax.all_to_all(own_keys.reshape(devices, capacity, SEG_LEN, columns), 'sp...  13.9 us
    psum x1, blocking collectives, body(): key_totals = lax.psum(squares(encoded), 'head')  11.9 us
    psum x1, blocking collectives, body(): totals = lax.psum(squares(flat_self), 'head')  11.9 us
    all_to_all x1, blocking collectives, body(): lax.all_to_all(request, 'span', split_axis=0, concat_axis=0, tiled=True)  9.68 us
    dot_general x3, matrix products, attend(): jnp.einsum('bqhd,bkhd->bhqk', query_heads, key_heads, preferred_element_t...  5.02 us
    sub x3, other arithmetic, attend(): logit_scores = logit_scores - jnp.max(logit_scores, axis=-1, keepdims=True)  4.37 us
  transfers between devices with their start and end apart: 4, of which 2 were waited for; matrix products, arithmetic and copies ran while one was open for 25% of the time, Pallas kernels for 0%

commit v1 on v0

--- a/solution.py
+++ b/solution.py
@@ -1,6 +1,10 @@
+import functools
+
 import jax
 import jax.numpy as jnp
 from jax import lax
+from jax.experimental import pallas as pl
+from jax.experimental.pallas import tpu as pltpu
 from jax.sharding import PartitionSpec as P
 
 HEAD_DIM = 128
@@ -117,6 +121,332 @@
     return blended.reshape(SEG_DEV * SEG_LEN, columns)
 
 
+MESH = pl.DeviceIdType.MESH
+GROUPS = 4
+
+
+def dot_t(a, b):
+    return lax.dot_general(a, b, (((1,), (1,)), ((), ())), preferred_element_type=jnp.float32)
+
+
+def dot(a, b):
+    return lax.dot_general(a, b, (((1,), (0,)), ((), ())), preferred_element_type=jnp.float32)
+
+
+def kernel(
+    heads_axis, full_width,
+    src_ref, nq_hbm, nk_hbm, nv_hbm, sk_hbm, sv_hbm, dq_hbm, out_ref,
+    nq, nk, nv, dq, *rest,
+):
+    kbufs, vbufs = rest[:GROUPS], rest[GROUPS:2 * GROUPS]
+    (own_out, enc, squares_acc, row_scale, key_scale,
+     stat1, stat2, peer1, peer2, behind2,
+     in_sem, dq_sem, local_sem, send_sem, recv_sem,
+     stat_send, stat_recv, prior_send, prior_recv) = rest[2 * GROUPS:]
+    per_device = nq.shape[0]
+    seg_dev = dq.shape[0]
+    columns = nq.shape[2]
+    width = columns // GROUPS
+    group_heads = width // HEAD_DIM
+    span = lax.axis_size("span")
+    me = lax.axis_index("span")
+    lane = lax.axis_index("head")
+    core, across, along = me ^ 1, me ^ 2, me ^ 4
+    after = lax.rem(me + 1, span)
+    before = lax.rem(me + span - 1, span)
+    softmax_scale = HEAD_DIM ** (-0.5)
+
+    for i in range(per_device):
+        for a, (hbm, vm) in enumerate(((nq_hbm, nq), (nk_hbm, nk), (nv_hbm, nv))):
+            pltpu.make_async_copy(hbm.at[i], vm.at[i], in_sem.at[a, i]).start()
+    dq_copy = pltpu.make_async_copy(dq_hbm, dq, dq_sem)
+    dq_copy.start()
+
+    barrier = pltpu.get_barrier_semaphore()
+    greeted = 0
+    for target in (core, across, along):
+        pl.semaphore_signal(barrier, inc=1, device_id={"span": target, "head": lane}, device_id_type=MESH)
+        greeted += 1
+    for k in range(1, heads_axis):
+        other = lax.rem(lane + k, heads_axis)
+        pl.semaphore_signal(barrier, inc=1, device_id={"span": me, "head": other}, device_id_type=MESH)
+        greeted += 1
+    for k in range(heads_axis):
+        other = lax.rem(lane + k, heads_axis)
+        for target in (after, before):
+            pl.semaphore_signal(barrier, inc=1, device_id={"span": target, "head": other}, device_id_type=MESH)
+            greeted += 1
+    pl.semaphore_wait(barrier, greeted)
+
+    chunks = 2 * GROUPS
+
+    def buffer(j):
+        return (kbufs, vbufs)[j % 2][j // 2]
+
+    def source(j):
+        hbm = (sk_hbm, sv_hbm)[j % 2]
+        return hbm.at[:, :, pl.ds((j // 2) * width, width)]
+
+    def block(j, owner):
+        return buffer(j).at[pl.ds(owner * seg_dev, seg_dev)]
+
+    def half(j, owner, part):
+        rows = seg_dev // 2
+        return buffer(j).at[pl.ds(owner * seg_dev + part * rows, rows)]
+
+    sent = {}
+
+    def push(kind, j, src, dst, target):
+        copy = pltpu.make_async_remote_copy(
+            src_ref=src, dst_ref=dst, send_sem=send_sem.at[kind, j], recv_sem=recv_sem.at[kind, j],
+            device_id={"span": target, "head": lane}, device_id_type=MESH)
+        copy.start()
+        sent[kind, j] = copy
+
+    def direct(j):
+        push(0, j, source(j), block(j, me), across)
+        push(1, j, source(j), block(j, me), along)
+
+    local = []
+    direct(0)
+    direct(1)
+    for j in range(chunks):
+        push(4, j, source(j), block(j, me), core)
+        copy = pltpu.make_async_copy(source(j), block(j, me), local_sem.at[j])
+        copy.start()
+        local.append(copy)
+
+    def forward(j):
+        sent[2, j].wait_recv()
+        sent[3, j].wait_recv()
+        push(7, j, block(j, me ^ 6), block(j, me ^ 6), core)
+
+    def step(j):
+        sent[1, j].wait_recv()
+        push(2, j, half(j, along, 0), half(j, along, 0), across)
+        sent[0, j].wait_recv()
+        push(3, j, half(j, across, 1), half(j, across, 1), along)
+        if j + 2 < chunks:
+            direct(j + 2)
+        push(5, j, block(j, across), block(j, across), core)
+        push(6, j, block(j, along), block(j, along), core)
+        if j >= 1:
+            forward(j - 1)
+
+    def arrived(j):
+        local[j].wait()
+        for kind in (4, 5, 6, 7):
+            sent[kind, j].wait_recv()
+
+    ones = jnp.ones((NBR_LEN, HEAD_DIM), jnp.bfloat16)
+
+    def self_step(i, carry):
+        for a, (hbm, vm) in enumerate(((nq_hbm, nq), (nk_hbm, nk), (nv_hbm, nv))):
+            pltpu.make_async_copy(hbm.at[i], vm.at[i], in_sem.at[a, i]).wait()
+        total = jnp.zeros((NBR_LEN, HEAD_DIM), jnp.float32)
+        for h in range(columns // HEAD_DIM):
+            cols = pl.ds(h * HEAD_DIM, HEAD_DIM)
+            scores = dot_t(nq[i, :, cols], nk[i, :, cols]) * softmax_scale
+            weights = jnp.exp(scores - jnp.max(scores, axis=-1, keepdims=True)).astype(jnp.bfloat16)
+            o = (dot(weights, nv[i, :, cols]) / dot(weights, ones)).astype(jnp.bfloat16)
+            own_out[h // group_heads, i, :, pl.ds((h % group_heads) * HEAD_DIM, HEAD_DIM)] = o
+            wide = o.astype(jnp.float32)
+            total = total + wide * wide
+        stat1[pl.ds(i, 1), :] = jnp.sum(total.T, axis=0, keepdims=True)
+        return carry
+
+    def exchange(kind, stat, peer):
+        out = []
+        for k in range(1, heads_axis):
+            other = lax.rem(lane + k, heads_axis)
+            copy = pltpu.make_async_remote_copy(
+                src_ref=stat, dst_ref=peer.at[k - 1],
+                send_sem=stat_send.at[kind, k - 1], recv_sem=stat_recv.at[kind, k - 1],
+                device_id={"span": me, "head": other}, device_id_type=MESH)
+            copy.start()
+            out.append(copy)
+        return out
+
+    def cross_step(g, i):
+        kb, vb = kbufs[g], vbufs[g]
+        segment = src_ref[i]
+        scale = row_scale[i, :, :SEG_LEN]
+        key_rows = kb[segment]
+        value_rows = vb[segment]
+        total = jnp.zeros((NBR_LEN, HEAD_DIM), jnp.float32)
+        for h in range(group_heads):
+            lo, hi = h * HEAD_DIM, (h + 1) * HEAD_DIM
+            first = own_out[g, i, :, pl.ds(lo, HEAD_DIM)]
+            scores = dot_t(first, key_rows[:, lo:hi]) * scale
+            weights = jnp.exp(scores - jnp.max(scores, axis=-1, keepdims=True)).astype(jnp.bfloat16)
+            crossed = (dot(weights, value_rows[:, lo:hi]) / dot(weights, ones[:SEG_LEN])).astype(jnp.bfloat16)
+            both = (first.astype(jnp.float32) + crossed.astype(jnp.float32)).astype(jnp.bfloat16)
+            enc[g, NEIGHBOURS + i, :, pl.ds(lo, HEAD_DIM)] = both
+            wide = both.astype(jnp.float32)
+            total = total + wide * wide
+        if g > 0:
+            total = total + squares_acc[i]
+        if g < GROUPS - 1:
+            squares_acc[i] = total
+        else:
+            stat2[pl.ds(i, 1), :] = jnp.sum(total.T, axis=0, keepdims=True)
+
+    prior = []
+
+    def cross(g):
+        arrived(2 * g)
+        arrived(2 * g + 1)
+        for i in range(per_device - NEIGHBOURS, per_device):
+            cross_step(g, i)
+        copy = pltpu.make_async_remote_copy(
+            src_ref=enc.at[g, pl.ds(per_device, NEIGHBOURS)], dst_ref=enc.at[g, pl.ds(0, NEIGHBOURS)],
+            send_sem=prior_send.at[g], recv_sem=prior_recv.at[g],
+            device_id={"span": after, "head": lane}, device_id_type=MESH)
+        copy.start()
+        prior.append(copy)
+
+        def rest_step(t, carry):
+            for b in range(2):
+                cross_step(g, 2 * t + b)
+            return carry
+
+        lax.fori_loop(0, (per_device - NEIGHBOURS) // 2, rest_step, 0)
+
+    quarter = per_device // 4
+    for j in range(4):
+        lax.fori_loop(j * quarter, (j + 1) * quarter, self_step, 0)
+        step(j)
+    first_stats = exchange(0, stat1, peer1)
+    step(4)
+    for copy in first_stats:
+        copy.wait_recv()
+    total1 = stat1[...]
+    for k in range(heads_axis - 1):
+        total1 = total1 + peer1[k]
+    total1 = lax.rsqrt(total1 / full_width + epsilon) * softmax_scale
+    for i in range(per_device):
+        row_scale[i] = jnp.broadcast_to(total1[i:i + 1], (NBR_LEN, NBR_LEN)).T
+    cross(0)
+    step(5)
+    step(6)
+    cross(1)
+    step(7)
+    cross(2)
+    forward(7)
+    cross(3)
+
+    second_stats = exchange(1, stat2, peer2)
+    behind_stats = []
+    for k in range(heads_axis):
+        other = lax.rem(lane + k, heads_axis)
+        copy = pltpu.make_async_remote_copy(
+            src_ref=stat2, dst_ref=behind2.at[k],
+            send_sem=stat_send.at[2, k], recv_sem=stat_recv.at[2, k],
+            device_id={"span": after, "head": other}, device_id_type=MESH)
+        copy.start()
+        behind_stats.append(copy)
+    dq_copy.wait()
+    for copy in second_stats:
+        copy.wait_recv()
+    total2 = stat2[...]
+    for k in range(heads_axis - 1):
+        total2 = total2 + peer2[k]
+    key_scale[pl.ds(NEIGHBOURS, per_device), :] = lax.rsqrt(total2 / full_width + epsilon) * softmax_scale
+
+    def decode_step(u, carry):
+        scales = [key_scale[pl.ds(NEIGHBOURS * u + n, 1), :] for n in range(NEIGHBOURS)]
+        scale = jnp.concatenate(scales, axis=1)
+        for h in range(columns // HEAD_DIM):
+            g, cols = h // group_heads, pl.ds((h % group_heads) * HEAD_DIM, HEAD_DIM)
+            rows = enc[g, pl.ds(NEIGHBOURS * u, NEIGHBOURS), :, cols].reshape(NEIGHBOURS * NBR_LEN, HEAD_DIM)
+            scores = dot_t(dq[u, :, pl.ds(h * HEAD_DIM, HEAD_DIM)], rows) * scale
+            weights = jnp.exp(scores - jnp.max(scores, axis=-1, keepdims=True)).astype(jnp.bfloat16)
+            norm = jnp.sum(weights.astype(jnp.float32), axis=-1, keepdims=True)
+            out_ref[u, :, pl.ds(h * HEAD_DIM, HEAD_DIM)] = (dot(weights, rows) / norm).astype(jnp.bfloat16)
+        return carry
+
+    lax.fori_loop(1, seg_dev, decode_step, 0)
+    for copy in behind_stats:
+        copy.wait_recv()
+    for copy in prior:
+        copy.wait_recv()
+    total3 = behind2[0]
+    for k in range(1, heads_axis):
+        total3 = total3 + behind2[k]
+    total3 = lax.rsqrt(total3 / full_width + epsilon) * softmax_scale
+    key_scale[pl.ds(0, NEIGHBOURS), :] = total3[per_device - NEIGHBOURS:]
+
+    @pl.when(me == 0)
+    def _():
+        enc[:, pl.ds(0, NEIGHBOURS)] = jnp.zeros((GROUPS, NEIGHBOURS, NBR_LEN, width), jnp.bfloat16)
+
+    decode_step(0, 0)
+    for copy in list(sent.values()) + prior + first_stats + second_stats + behind_stats:
+        copy.wait_send()
+
+
+def fused_body(
+    neighbour_query,
+    neighbour_key,
+    neighbour_value,
+    segment_key,
+    segment_value,
+    decoder_query,
+    sources,
+):
+    columns = neighbour_query.shape[1]
+    heads_axis = lax.axis_size("head")
+    span = lax.axis_size("span")
+    per_device = SEG_DEV * NEIGHBOURS
+    width = columns // GROUPS
+    bf16, f32 = jnp.bfloat16, jnp.float32
+    neighbour_shape = (per_device, NBR_LEN, columns)
+    segment_shape = (SEG_DEV, SEG_LEN, columns)
+    chunks = 2 * GROUPS
+    any_space = pl.BlockSpec(memory_space=pl.ANY)
+    dma = pltpu.SemaphoreType.DMA
+    out = pl.pallas_call(
+        functools.partial(kernel, heads_axis, columns * heads_axis),
+        out_shape=jax.ShapeDtypeStruct(segment_shape, bf16),
+        in_specs=[pl.BlockSpec(memory_space=pltpu.SMEM)] + [any_space] * 6,
+        out_specs=pl.BlockSpec(memory_space=pltpu.VMEM),
+        scratch_shapes=[pltpu.VMEM(neighbour_shape, bf16)] * 3
+        + [pltpu.VMEM(segment_shape, bf16)]
+        + [pltpu.VMEM((span * SEG_DEV, SEG_LEN, width), bf16)] * chunks
+        + [
+            pltpu.VMEM((GROUPS, per_device, NBR_LEN, width), bf16),
+            pltpu.VMEM((GROUPS, per_device + NEIGHBOURS, NBR_LEN, width), bf16),
+            pltpu.VMEM((per_device, NBR_LEN, HEAD_DIM), f32),
+            pltpu.VMEM((per_device, NBR_LEN, NBR_LEN), f32),
+            pltpu.VMEM((per_device + NEIGHBOURS, NBR_LEN), f32),
+            pltpu.VMEM((per_device, NBR_LEN), f32),
+            pltpu.VMEM((per_device, NBR_LEN), f32),
+            pltpu.VMEM((heads_axis - 1, per_device, NBR_LEN), f32),
+            pltpu.VMEM((heads_axis - 1, per_device, NBR_LEN), f32),
+            pltpu.VMEM((heads_axis, per_device, NBR_LEN), f32),
+            dma((3, per_device)),
+            dma,
+            dma((chunks,)),
+            dma((8, chunks)),
+            dma((8, chunks)),
+            dma((3, heads_axis)),
+            dma((3, heads_axis)),
+            dma((GROUPS,)),
+            dma((GROUPS,)),
+        ],
+        compiler_params=pltpu.CompilerParams(collective_id=0, has_side_effects=True),
+    )(
+        sources.reshape(per_device),
+        neighbour_query.reshape(neighbour_shape),
+        neighbour_key.reshape(neighbour_shape),
+        neighbour_value.reshape(neighbour_shape),
+        segment_key.reshape(segment_shape),
+        segment_value.reshape(segment_shape),
+        decoder_query.reshape(segment_shape),
+    )
+    return out.reshape(SEG_DEV * SEG_LEN, columns)
+
+
 def solution(mesh):
     placed = (
         P("span", "head"),
@@ -127,6 +457,7 @@
         P("span", "head"),
         P("span", None),
     )
+    cube = mesh.shape["span"] == 2 * 2 * 2
     return jax.shard_map(
-        body, mesh=mesh, in_specs=placed, out_specs=P("span", "head"), check_vma=False
+        fused_body if cube else body, mesh=mesh, in_specs=placed, out_specs=P("span", "head"), check_vma=False
     )

time: 127 us -> 68.1 us (0.54)
  Pallas kernels: 0 us -> 64.7 us
  blocking collectives: 33.5 us -> 0 us
  local copies, waits for them, and re-layouts: 32.6 us -> 3.23 us
  matrix products: 20.4 us -> 0 us
  waiting for transfers between devices: 17.1 us -> 0 us
  starting transfers between devices: 12.1 us -> 0 us
  other arithmetic: 10.2 us -> 0 us
    pallas_call x0 -> x1, Pallas kernels: none -> 64.7 us  [fused_body(): pl.pallas_call(functools.partial(kernel, heads_axis, columns * heads_axis...]
    psum x2 -> x0, blocking collectives: 23.9 us -> none  [the longest x1 11.9 us: body(): key_totals = lax.psum(squares(encoded), 'head')]
    dot_general x6 -> x0, matrix products: 20.4 us -> none  [the longest x3 15.4 us: attend(): jnp.einsum('bhqk,bkhd->bqhd', weights, value_heads, preferred_element_typ...]
    all_to_all x2 -> x0, waiting for transfers between devices: 17.1 us -> none  [the longest x1 13.9 us: body(): lax.all_to_all(own_keys.reshape(devices, capacity, SEG_LEN, columns), 'sp...]
    unnamed x30 -> x2, local copies, waits for them, and re-layouts: 15.8 us -> 2.63 us
    all_to_all x1 -> x0, blocking collectives: 9.68 us -> none  [body(): lax.all_to_all(request, 'span', split_axis=0, concat_axis=0, tiled=True)]
    gather x4 -> x0, local copies, waits for them, and re-layouts: 8.87 us -> none  [the longest x1 3.19 us: body(): got_values.reshape(devices * capacity, SEG_LEN, columns)[slots]]
    all_to_all x2 -> x0, starting transfers between devices: 7.94 us -> none  [the longest x1 4.33 us: body(): lax.all_to_all(own_values.reshape(devices, capacity, SEG_LEN, columns), '...]
  transfers between devices with their start and end apart: 4 -> 0, of which waited for: 2 -> 0; matrix products, arithmetic and copies ran while one was open for 25% -> 0% of each run, Pallas kernels for 0% -> 0%
where the time goes in v1:
time: 68.1 us; the launch traced here: 67.9 us
  Pallas kernels  64.7 us (95%)
  local copies, waits for them, and re-layouts  3.23 us (5%)
    pallas_call x1, Pallas kernels, fused_body(): pl.pallas_call(functools.partial(kernel, heads_axis, columns * heads_axis...  64.7 us
    unnamed x2, local copies, waits for them, and re-layouts  2.63 us

profile of v1, /device:TPU:0, one launch (start us, length us, event | category | flops | bytes accessed | tf_op | source)
XLA Modules:
  0.0 67.9 jit_solution(17886285967826374830)
XLA Ops:
  0.0 0.8 %copy.9 = s32[4,2]{1,0:T(4,128)S(1)} copy(s32[4,2]{0,1:T(2,128)} %param.13) | data formatting | bytes 64 | tf_op args[6]
  0.8 0.6 reshape.24.src_ref
  1.4 64.7 %shard_map.73 = bf16[4,64,1024]{2,1,0:T(8,128)(2,1)} custom-call(s32[8]{0:T(128)} %reshape.24.src_ref, bf16[8,128,1024]{2,1,0:T(8,128)(2,1)} %bitcast.8, bf16[8,128,1024]{2,1,0:T(8,128)(2,1)} %bitcast.9, bf16[8,128,1024]{2,1,0:T(8,128)(2,1)} %bitcast.10, bf16[4,64,1024]{2,1,0:T(8,128)(2,1)} %bitcast.11, bf16[4,64,1024]{2,1,0:T(8,128)(2,1)} %bitcast.12, ...), custom_call_target="tpu_custom_call" | custom-call | tf_op jit(solution)/shard_map/pallas_call | solution.py:408
  66.0 1.9 %copy.11 = bf16[256,1024]{1,0:T(8,128)(2,1)} copy(bf16[256,1024]{1,0:T(8,128)(2,1)} %bitcast.7) | data formatting | bytes 1048576

commit v2 on v1

--- a/solution.py
+++ b/solution.py
@@ -139,7 +139,7 @@
     nq, nk, nv, dq, *rest,
 ):
     kbufs, vbufs = rest[:GROUPS], rest[GROUPS:2 * GROUPS]
-    (own_out, enc, squares_acc, row_scale, key_scale,
+    (own_out, mixing, enc, squares_acc, row_scale, key_scale,
      stat1, stat2, peer1, peer2, behind2,
      in_sem, dq_sem, local_sem, send_sem, recv_sem,
      stat_send, stat_recv, prior_send, prior_recv) = rest[2 * GROUPS:]
@@ -181,11 +181,11 @@
     chunks = 2 * GROUPS
 
     def buffer(j):
-        return (kbufs, vbufs)[j % 2][j // 2]
+        return (kbufs + vbufs)[j]
 
     def source(j):
-        hbm = (sk_hbm, sv_hbm)[j % 2]
-        return hbm.at[:, :, pl.ds((j // 2) * width, width)]
+        hbm = (sk_hbm, sv_hbm)[j // GROUPS]
+        return hbm.at[:, :, pl.ds((j % GROUPS) * width, width)]
 
     def block(j, owner):
         return buffer(j).at[pl.ds(owner * seg_dev, seg_dev)]
@@ -208,9 +208,8 @@
         push(1, j, source(j), block(j, me), along)
 
     local = []
-    direct(0)
-    direct(1)
     for j in range(chunks):
+        direct(j)
         push(4, j, source(j), block(j, me), core)
         copy = pltpu.make_async_copy(source(j), block(j, me), local_sem.at[j])
         copy.start()
@@ -226,12 +225,8 @@
         push(2, j, half(j, along, 0), half(j, along, 0), across)
         sent[0, j].wait_recv()
         push(3, j, half(j, across, 1), half(j, across, 1), along)
-        if j + 2 < chunks:
-            direct(j + 2)
         push(5, j, block(j, across), block(j, across), core)
         push(6, j, block(j, along), block(j, along), core)
-        if j >= 1:
-            forward(j - 1)
 
     def arrived(j):
         local[j].wait()
@@ -267,19 +262,33 @@
             out.append(copy)
         return out
 
+    def weigh_step(g, i):
+        key_rows = kbufs[g][src_ref[i // NEIGHBOURS, i % NEIGHBOURS]]
+        scale = row_scale[i, :, :SEG_LEN]
+        for h in range(group_heads):
+            lo, hi = h * HEAD_DIM, (h + 1) * HEAD_DIM
+            scores = dot_t(own_out[g, i, :, pl.ds(lo, HEAD_DIM)], key_rows[:, lo:hi]) * scale
+            weights = jnp.exp(scores - jnp.max(scores, axis=-1, keepdims=True))
+            weights = weights / jnp.sum(weights, axis=-1, keepdims=True)
+            mixing[g, i, h] = weights.astype(jnp.bfloat16)
+
+    def weigh(g):
+        arrived(g)
+
+        def pair_step(t, carry):
+            for b in range(2):
+                weigh_step(g, 2 * t + b)
+            return carry
+
+        lax.fori_loop(0, per_device // 2, pair_step, 0)
+
     def cross_step(g, i):
-        kb, vb = kbufs[g], vbufs[g]
-        segment = src_ref[i]
-        scale = row_scale[i, :, :SEG_LEN]
-        key_rows = kb[segment]
-        value_rows = vb[segment]
+        value_rows = vbufs[g][src_ref[i // NEIGHBOURS, i % NEIGHBOURS]]
         total = jnp.zeros((NBR_LEN, HEAD_DIM), jnp.float32)
         for h in range(group_heads):
             lo, hi = h * HEAD_DIM, (h + 1) * HEAD_DIM
             first = own_out[g, i, :, pl.ds(lo, HEAD_DIM)]
-            scores = dot_t(first, key_rows[:, lo:hi]) * scale
-            weights = jnp.exp(scores - jnp.max(scores, axis=-1, keepdims=True)).astype(jnp.bfloat16)
-            crossed = (dot(weights, value_rows[:, lo:hi]) / dot(weights, ones[:SEG_LEN])).astype(jnp.bfloat16)
+            crossed = dot(mixing[g, i, h], value_rows[:, lo:hi]).astype(jnp.bfloat16)
             both = (first.astype(jnp.float32) + crossed.astype(jnp.float32)).astype(jnp.bfloat16)
             enc[g, NEIGHBOURS + i, :, pl.ds(lo, HEAD_DIM)] = both
             wide = both.astype(jnp.float32)
@@ -294,8 +303,7 @@
     prior = []
 
     def cross(g):
-        arrived(2 * g)
-        arrived(2 * g + 1)
+        arrived(GROUPS + g)
         for i in range(per_device - NEIGHBOURS, per_device):
             cross_step(g, i)
         copy = pltpu.make_async_remote_copy(
@@ -315,9 +323,11 @@
     quarter = per_device // 4
     for j in range(4):
         lax.fori_loop(j * quarter, (j + 1) * quarter, self_step, 0)
-        step(j)
+        if j > 0:
+            step(2 * j - 2)
+            step(2 * j - 1)
     first_stats = exchange(0, stat1, peer1)
-    step(4)
+    step(6)
     for copy in first_stats:
         copy.wait_recv()
     total1 = stat1[...]
@@ -326,14 +336,15 @@
     total1 = lax.rsqrt(total1 / full_width + epsilon) * softmax_scale
     for i in range(per_device):
         row_scale[i] = jnp.broadcast_to(total1[i:i + 1], (NBR_LEN, NBR_LEN)).T
-    cross(0)
-    step(5)
-    step(6)
-    cross(1)
     step(7)
-    cross(2)
-    forward(7)
-    cross(3)
+    forward(0)
+    for g in range(GROUPS):
+        forward(g + 1)
+        weigh(g)
+    for g in range(GROUPS):
+        if g + 1 < GROUPS:
+            forward(GROUPS + 1 + g)
+        cross(g)
 
     second_stats = exchange(1, stat2, peer2)
     behind_stats = []
@@ -403,7 +414,7 @@
     neighbour_shape = (per_device, NBR_LEN, columns)
     segment_shape = (SEG_DEV, SEG_LEN, columns)
     chunks = 2 * GROUPS
-    any_space = pl.BlockSpec(memory_space=pl.ANY)
+    any_space = pl.BlockSpec(memory_space=pltpu.HBM)
     dma = pltpu.SemaphoreType.DMA
     out = pl.pallas_call(
         functools.partial(kernel, heads_axis, columns * heads_axis),
@@ -415,6 +426,7 @@
         + [pltpu.VMEM((span * SEG_DEV, SEG_LEN, width), bf16)] * chunks
         + [
             pltpu.VMEM((GROUPS, per_device, NBR_LEN, width), bf16),
+            pltpu.VMEM((GROUPS, per_device, width // HEAD_DIM, NBR_LEN, SEG_LEN), bf16),
             pltpu.VMEM((GROUPS, per_device + NEIGHBOURS, NBR_LEN, width), bf16),
             pltpu.VMEM((per_device, NBR_LEN, HEAD_DIM), f32),
             pltpu.VMEM((per_device, NBR_LEN, NBR_LEN), f32),
@@ -434,9 +446,10 @@
             dma((GROUPS,)),
             dma((GROUPS,)),
         ],
-        compiler_params=pltpu.CompilerParams(collective_id=0, has_side_effects=True),
+        compiler_params=pltpu.CompilerParams(
+            collective_id=0, has_side_effects=True, vmem_limit_bytes=40 * 1024 * 1024),
     )(
-        sources.reshape(per_device),
+        sources,
         neighbour_query.reshape(neighbour_shape),
         neighbour_key.reshape(neighbour_shape),
         neighbour_value.reshape(neighbour_shape),

time: 68.1 us -> 67.8 us (level)
  Pallas kernels: 64.7 us -> 58 us
  local copies, waits for them, and re-layouts: 3.23 us -> 9.45 us
    unnamed x2 -> x14, local copies, waits for them, and re-layouts: 2.63 us -> 9.45 us
    pallas_call x1, Pallas kernels: 64.7 us -> 58 us  [fused_body(): pl.pallas_call(functools.partial(kernel, heads_axis, columns * heads_axis...]
where the time goes in v2:
time: 67.8 us; the launch traced here: 67.4 us
  Pallas kernels  58 us (86%)
  local copies, waits for them, and re-layouts  9.45 us (14%)
    pallas_call x1, Pallas kernels, fused_body(): pl.pallas_call(functools.partial(kernel, heads_axis, columns * heads_axis...  58 us
    unnamed x14, local copies, waits for them, and re-layouts  9.45 us

profile of v2, /device:TPU:0, one launch (start us, length us, event | category | flops | bytes accessed | tf_op | source)
XLA Modules:
  0.0 67.4 jit_solution(3437009639003162067)
XLA Ops:
  0.0 0.8 %copy.8.src_ref = s32[4,2]{1,0:T(4,128)S(1)} copy(s32[4,2]{0,1:T(2,128)} %param.13) | data formatting | bytes 64 | tf_op args[6]
  0.8 0.0 copy-start
  0.8 1.6 %copy-done = bf16[1024,1024]{1,0:T(8,128)(2,1)S(1)} copy-done((bf16[1024,1024]{1,0:T(8,128)(2,1)S(1)}, bf16[1024,1024]{1,0:T(8,128)(2,1)}, u32[]{:S(2)}) %copy-start) | copy-done | bytes 2097176
  2.4 0.0 copy-start.1
  2.4 1.6 %copy-done.1 = bf16[1024,1024]{1,0:T(8,128)(2,1)S(1)} copy-done((bf16[1024,1024]{1,0:T(8,128)(2,1)S(1)}, bf16[1024,1024]{1,0:T(8,128)(2,1)}, u32[]{:S(2)}) %copy-start.1) | copy-done | bytes 2097176
  3.9 0.0 copy-start.2
  4.0 1.6 %copy-done.2 = bf16[1024,1024]{1,0:T(8,128)(2,1)S(1)} copy-done((bf16[1024,1024]{1,0:T(8,128)(2,1)S(1)}, bf16[1024,1024]{1,0:T(8,128)(2,1)}, u32[]{:S(2)}) %copy-start.2) | copy-done | bytes 2097176
  5.5 0.0 copy-start.3
  5.5 1.0 %copy-done.3 = bf16[256,1024]{1,0:T(8,128)(2,1)S(1)} copy-done((bf16[256,1024]{1,0:T(8,128)(2,1)S(1)}, bf16[256,1024]{1,0:T(8,128)(2,1)}, u32[]{:S(2)}) %copy-start.3) | copy-done | bytes 524312
  6.6 0.0 copy-start.4
  6.6 1.0 %copy-done.4 = bf16[256,1024]{1,0:T(8,128)(2,1)S(1)} copy-done((bf16[256,1024]{1,0:T(8,128)(2,1)S(1)}, bf16[256,1024]{1,0:T(8,128)(2,1)}, u32[]{:S(2)}) %copy-start.4) | copy-done | bytes 524312
  7.6 0.0 copy-start.5
  7.6 1.0 %copy-done.5 = bf16[256,1024]{1,0:T(8,128)(2,1)S(1)} copy-done((bf16[256,1024]{1,0:T(8,128)(2,1)S(1)}, bf16[256,1024]{1,0:T(8,128)(2,1)}, u32[]{:S(2)}) %copy-start.5) | copy-done | bytes 524312
  8.7 58.0 %shard_map.73 = bf16[4,64,1024]{2,1,0:T(8,128)(2,1)S(1)} custom-call(s32[4,2]{1,0:T(4,128)S(1)} %copy.8.src_ref, bf16[8,128,1024]{2,1,0:T(8,128)(2,1)S(1)} %bitcast.7, bf16[8,128,1024]{2,1,0:T(8,128)(2,1)S(1)} %bitcast.8, bf16[8,128,1024]{2,1,0:T(8,128)(2,1)S(1)} %bitcast.9, bf16[4,64,1024]{2,1,0:T(8,128)(2,1)S(1)} %bitcast.11, ...), custom_call_target="tpu_custom_call" | custom-call | tf_op jit(solution)/shard_map/pallas_call | solution.py:419
  66.6 0.8 %copy.10 = bf16[256,1024]{1,0:T(8,128)(2,1)} copy(bf16[256,1024]{1,0:T(8,128)(2,1)S(1)} %bitcast.10) | data formatting | bytes 1048576
Async XLA Ops:
  0.8 1.6 %copy-start = (bf16[1024,1024]{1,0:T(8,128)(2,1)S(1)}, bf16[1024,1024]{1,0:T(8,128)(2,1)}, u32[]{:S(2)}) copy-start(bf16[1024,1024]{1,0:T(8,128)(2,1)} %param.7) | copy-start | bytes 6291460
  2.4 1.6 %copy-start.1 = (bf16[1024,1024]{1,0:T(8,128)(2,1)S(1)}, bf16[1024,1024]{1,0:T(8,128)(2,1)}, u32[]{:S(2)}) copy-start(bf16[1024,1024]{1,0:T(8,128)(2,1)} %param.8) | copy-start | bytes 6291460
  3.9 1.6 %copy-start.2 = (bf16[1024,1024]{1,0:T(8,128)(2,1)S(1)}, bf16[1024,1024]{1,0:T(8,128)(2,1)}, u32[]{:S(2)}) copy-start(bf16[1024,1024]{1,0:T(8,128)(2,1)} %param.9) | copy-start | bytes 6291460
  5.5 1.0 %copy-start.3 = (bf16[256,1024]{1,0:T(8,128)(2,1)S(1)}, bf16[256,1024]{1,0:T(8,128)(2,1)}, u32[]{:S(2)}) copy-start(bf16[256,1024]{1,0:T(8,128)(2,1)} %param.10) | copy-start | bytes 1572868
  6.6 1.0 %copy-start.4 = (bf16[256,1024]{1,0:T(8,128)(2,1)S(1)}, bf16[256,1024]{1,0:T(8,128)(2,1)}, u32[]{:S(2)}) copy-start(bf16[256,1024]{1,0:T(8,128)(2,1)} %param.11) | copy-start | bytes 1572868
  7.6 1.0 %copy-start.5 = (bf16[256,1024]{1,0:T(8,128)(2,1)S(1)}, bf16[256,1024]{1,0:T(8,128)(2,1)}, u32[]{:S(2)}) copy-start(bf16[256,1024]{1,0:T(8,128)(2,1)} %param.12) | copy-start | bytes 1572868

commit v3 on v2

--- a/solution.py
+++ b/solution.py
@@ -1,4 +1,5 @@
 import functools
+import math
 
 import jax
 import jax.numpy as jnp
@@ -129,8 +130,24 @@
     return lax.dot_general(a, b, (((1,), (1,)), ((), ())), preferred_element_type=jnp.float32)
 
 
-def dot(a, b):
-    return lax.dot_general(a, b, (((1,), (0,)), ((), ())), preferred_element_type=jnp.float32)
+def dot_first(a, b):
+    return lax.dot_general(a, b, (((0,), (0,)), ((), ())), preferred_element_type=jnp.float32)
+
+
+def apart(rows):
+    count = rows.shape[1] // HEAD_DIM
+    zero = jnp.zeros((rows.shape[0], HEAD_DIM), rows.dtype)
+    lines = []
+    for h in range(count):
+        own = rows[:, h * HEAD_DIM:(h + 1) * HEAD_DIM]
+        lines.append(jnp.concatenate([own if k == h else zero for k in range(count)], axis=1))
+    return jnp.concatenate(lines, axis=0)
+
+
+def softmax(scores, axis):
+    weights = jnp.exp2(scores - jnp.max(scores, axis=axis, keepdims=True))
+    inverse = 1.0 / jnp.sum(weights, axis=axis, keepdims=True)
+    return (weights * inverse).astype(jnp.bfloat16)
 
 
 def kernel(
@@ -154,7 +171,7 @@
     core, across, along = me ^ 1, me ^ 2, me ^ 4
     after = lax.rem(me + 1, span)
     before = lax.rem(me + span - 1, span)
-    softmax_scale = HEAD_DIM ** (-0.5)
+    softmax_scale = HEAD_DIM ** (-0.5) / math.log(2.0)
 
     for i in range(per_device):
         for a, (hbm, vm) in enumerate(((nq_hbm, nq), (nk_hbm, nk), (nv_hbm, nv))):
@@ -233,17 +250,14 @@
         for kind in (4, 5, 6, 7):
             sent[kind, j].wait_recv()
 
-    ones = jnp.ones((NBR_LEN, HEAD_DIM), jnp.bfloat16)
-
     def self_step(i, carry):
         for a, (hbm, vm) in enumerate(((nq_hbm, nq), (nk_hbm, nk), (nv_hbm, nv))):
             pltpu.make_async_copy(hbm.at[i], vm.at[i], in_sem.at[a, i]).wait()
         total = jnp.zeros((NBR_LEN, HEAD_DIM), jnp.float32)
         for h in range(columns // HEAD_DIM):
             cols = pl.ds(h * HEAD_DIM, HEAD_DIM)
-            scores = dot_t(nq[i, :, cols], nk[i, :, cols]) * softmax_scale
-            weights = jnp.exp(scores - jnp.max(scores, axis=-1, keepdims=True)).astype(jnp.bfloat16)
-            o = (dot(weights, nv[i, :, cols]) / dot(weights, ones)).astype(jnp.bfloat16)
+            weights = softmax(dot_t(nk[i, :, cols], nq[i, :, cols]) * softmax_scale, 0)
+            o = dot_first(weights, nv[i, :, cols]).astype(jnp.bfloat16)
             own_out[h // group_heads, i, :, pl.ds((h % group_heads) * HEAD_DIM, HEAD_DIM)] = o
             wide = o.astype(jnp.float32)
             total = total + wide * wide
@@ -263,14 +277,10 @@
         return out
 
     def weigh_step(g, i):
-        key_rows = kbufs[g][src_ref[i // NEIGHBOURS, i % NEIGHBOURS]]
-        scale = row_scale[i, :, :SEG_LEN]
-        for h in range(group_heads):
-            lo, hi = h * HEAD_DIM, (h + 1) * HEAD_DIM
-            scores = dot_t(own_out[g, i, :, pl.ds(lo, HEAD_DIM)], key_rows[:, lo:hi]) * scale
-            weights = jnp.exp(scores - jnp.max(scores, axis=-1, keepdims=True))
-            weights = weights / jnp.sum(weights, axis=-1, keepdims=True)
-            mixing[g, i, h] = weights.astype(jnp.bfloat16)
+        keys = apart(kbufs[g][src_ref[i // NEIGHBOURS, i % NEIGHBOURS]])
+        scores = dot_t(keys, own_out[g, i]) * row_scale[pl.ds(i, 1), :]
+        weights = softmax(scores.reshape(group_heads, SEG_LEN, NBR_LEN), 1)
+        mixing[g, i] = weights.reshape(group_heads * SEG_LEN, NBR_LEN)
 
     def weigh(g):
         arrived(g)
@@ -283,16 +293,15 @@
         lax.fori_loop(0, per_device // 2, pair_step, 0)
 
     def cross_step(g, i):
-        value_rows = vbufs[g][src_ref[i // NEIGHBOURS, i % NEIGHBOURS]]
-        total = jnp.zeros((NBR_LEN, HEAD_DIM), jnp.float32)
-        for h in range(group_heads):
-            lo, hi = h * HEAD_DIM, (h + 1) * HEAD_DIM
-            first = own_out[g, i, :, pl.ds(lo, HEAD_DIM)]
-            crossed = dot(mixing[g, i, h], value_rows[:, lo:hi]).astype(jnp.bfloat16)
-            both = (first.astype(jnp.float32) + crossed.astype(jnp.float32)).astype(jnp.bfloat16)
-            enc[g, NEIGHBOURS + i, :, pl.ds(lo, HEAD_DIM)] = both
-            wide = both.astype(jnp.float32)
-            total = total + wide * wide
+        values = apart(vbufs[g][src_ref[i // NEIGHBOURS, i % NEIGHBOURS]])
+        crossed = dot_first(mixing[g, i], values).astype(jnp.bfloat16)
+        both = (own_out[g, i].astype(jnp.float32) + crossed.astype(jnp.float32)).astype(jnp.bfloat16)
+        enc[g, NEIGHBOURS + i] = both
+        wide = both.astype(jnp.float32)
+        wide = wide * wide
+        total = wide[:, :HEAD_DIM]
+        for h in range(1, group_heads):
+            total = total + wide[:, h * HEAD_DIM:(h + 1) * HEAD_DIM]
         if g > 0:
             total = total + squares_acc[i]
         if g < GROUPS - 1:
@@ -333,9 +342,7 @@
     total1 = stat1[...]
     for k in range(heads_axis - 1):
         total1 = total1 + peer1[k]
-    total1 = lax.rsqrt(total1 / full_width + epsilon) * softmax_scale
-    for i in range(per_device):
-        row_scale[i] = jnp.broadcast_to(total1[i:i + 1], (NBR_LEN, NBR_LEN)).T
+    row_scale[...] = lax.rsqrt(total1 / full_width + epsilon) * softmax_scale
     step(7)
     forward(0)
     for g in range(GROUPS):
@@ -365,15 +372,16 @@
     key_scale[pl.ds(NEIGHBOURS, per_device), :] = lax.rsqrt(total2 / full_width + epsilon) * softmax_scale
 
     def decode_step(u, carry):
-        scales = [key_scale[pl.ds(NEIGHBOURS * u + n, 1), :] for n in range(NEIGHBOURS)]
-        scale = jnp.concatenate(scales, axis=1)
-        for h in range(columns // HEAD_DIM):
-            g, cols = h // group_heads, pl.ds((h % group_heads) * HEAD_DIM, HEAD_DIM)
-            rows = enc[g, pl.ds(NEIGHBOURS * u, NEIGHBOURS), :, cols].reshape(NEIGHBOURS * NBR_LEN, HEAD_DIM)
-            scores = dot_t(dq[u, :, pl.ds(h * HEAD_DIM, HEAD_DIM)], rows) * scale
-            weights = jnp.exp(scores - jnp.max(scores, axis=-1, keepdims=True)).astype(jnp.bfloat16)
-            norm = jnp.sum(weights.astype(jnp.float32), axis=-1, keepdims=True)
-            out_ref[u, :, pl.ds(h * HEAD_DIM, HEAD_DIM)] = (dot(weights, rows) / norm).astype(jnp.bfloat16)
+        scale = jnp.concatenate([
+            jnp.broadcast_to(key_scale[pl.ds(NEIGHBOURS * u + n, 1), :], (NBR_LEN, NBR_LEN)).T
+            for n in range(NEIGHBOURS)], axis=0)
+        for g in range(GROUPS):
+            rows = enc[g, pl.ds(NEIGHBOURS * u, NEIGHBOURS)].reshape(NEIGHBOURS * NBR_LEN, width)
+            asked = apart(dq[u, :, pl.ds(g * width, width)])
+            out = dot_first(softmax(dot_t(rows, asked) * scale, 0), rows).astype(jnp.bfloat16)
+            for h in range(group_heads):
+                lo = h * HEAD_DIM
+                out_ref[u, :, pl.ds(g * width + lo, HEAD_DIM)] = out[h * SEG_LEN:(h + 1) * SEG_LEN, lo:lo + HEAD_DIM]
         return carry
 
     lax.fori_loop(1, seg_dev, decode_step, 0)
@@ -426,10 +434,10 @@
         + [pltpu.VMEM((span * SEG_DEV, SEG_LEN, width), bf16)] * chunks
         + [
             pltpu.VMEM((GROUPS, per_device, NBR_LEN, width), bf16),
-            pltpu.VMEM((GROUPS, per_device, width // HEAD_DIM, NBR_LEN, SEG_LEN), bf16),
+            pltpu.VMEM((GROUPS, per_device, width // HEAD_DIM * SEG_LEN, NBR_LEN), bf16),
             pltpu.VMEM((GROUPS, per_device + NEIGHBOURS, NBR_LEN, width), bf16),
             pltpu.VMEM((per_device, NBR_LEN, HEAD_DIM), f32),
-            pltpu.VMEM((per_device, NBR_LEN, NBR_LEN), f32),
+            pltpu.VMEM((per_device, NBR_LEN), f32),
             pltpu.VMEM((per_device + NEIGHBOURS, NBR_LEN), f32),
             pltpu.VMEM((per_device, NBR_LEN), f32),
             pltpu.VMEM((per_device, NBR_LEN), f32),
@@ -447,7 +455,7 @@
             dma((GROUPS,)),
         ],
         compiler_params=pltpu.CompilerParams(
-            collective_id=0, has_side_effects=True, vmem_limit_bytes=40 * 1024 * 1024),
+            collective_id=0, has_side_effects=True, vmem_limit_bytes=53 * 1024 * 1024),
     )(
         sources,
         neighbour_query.reshape(neighbour_shape),

time: 67.8 us -> 57.3 us (0.85)
  local copies, waits for them, and re-layouts: 9.45 us -> 1.56 us
  Pallas kernels: 58 us -> 55.6 us
    unnamed x14 -> x2, local copies, waits for them, and re-layouts: 9.45 us -> 1.56 us
    pallas_call x1, Pallas kernels: 58 us -> 55.6 us  [fused_body(): pl.pallas_call(functools.partial(kernel, heads_axis, columns * heads_axis...]
where the time goes in v3:
time: 57.3 us; the launch traced here: 57.2 us
  Pallas kernels  55.6 us (97%)
  local copies, waits for them, and re-layouts  1.56 us (3%)
    pallas_call x1, Pallas kernels, fused_body(): pl.pallas_call(functools.partial(kernel, heads_axis, columns * heads_axis...  55.6 us
    unnamed x2, local copies, waits for them, and re-layouts  1.56 us

profile of v3, /device:TPU:0, one launch (start us, length us, event | category | flops | bytes accessed | tf_op | source)
XLA Modules:
  0.0 57.2 jit_solution(18389259786881958316)
XLA Ops:
  0.0 0.8 %copy.8.src_ref = s32[4,2]{1,0:T(4,128)S(1)} copy(s32[4,2]{0,1:T(2,128)} %param.13) | data formatting | bytes 64 | tf_op args[6]
  0.8 55.6 %shard_map.73 = bf16[4,64,1024]{2,1,0:T(8,128)(2,1)S(1)} custom-call(s32[4,2]{1,0:T(4,128)S(1)} %copy.8.src_ref, bf16[8,128,1024]{2,1,0:T(8,128)(2,1)} %bitcast.8, bf16[8,128,1024]{2,1,0:T(8,128)(2,1)} %bitcast.9, bf16[8,128,1024]{2,1,0:T(8,128)(2,1)} %bitcast.10, bf16[4,64,1024]{2,1,0:T(8,128)(2,1)} %bitcast.11, bf16[4,64,1024]{2,1,0:T(8,128)(2,1)} %bitcast.12, ...), custom_call_target="tpu_custom_call" | custom-call | tf_op jit(solution)/shard_map/pallas_call | solution.py:427
  56.4 0.8 %copy.10 = bf16[256,1024]{1,0:T(8,128)(2,1)} copy(bf16[256,1024]{1,0:T(8,128)(2,1)S(1)} %bitcast.7) | data formatting | bytes 1048576

commit v4 on v3

--- a/solution.py
+++ b/solution.py
@@ -156,7 +156,7 @@
     nq, nk, nv, dq, *rest,
 ):
     kbufs, vbufs = rest[:GROUPS], rest[GROUPS:2 * GROUPS]
-    (own_out, mixing, enc, squares_acc, row_scale, key_scale,
+    (own_out, mixing, asked, enc, squares_acc, row_scale, key_scale,
      stat1, stat2, peer1, peer2, behind2,
      in_sem, dq_sem, local_sem, send_sem, recv_sem,
      stat_send, stat_recv, prior_send, prior_recv) = rest[2 * GROUPS:]
@@ -233,9 +233,9 @@
         local.append(copy)
 
     def forward(j):
-        sent[2, j].wait_recv()
-        sent[3, j].wait_recv()
-        push(7, j, block(j, me ^ 6), block(j, me ^ 6), core)
+        for part in range(2):
+            sent[2 + part, j].wait_recv()
+            push(7 + part, j, half(j, me ^ 6, part), half(j, me ^ 6, part), core)
 
     def step(j):
         sent[1, j].wait_recv()
@@ -247,20 +247,23 @@
 
     def arrived(j):
         local[j].wait()
-        for kind in (4, 5, 6, 7):
+        for kind in (4, 5, 6, 7, 8):
             sent[kind, j].wait_recv()
 
     def self_step(i, carry):
         for a, (hbm, vm) in enumerate(((nq_hbm, nq), (nk_hbm, nk), (nv_hbm, nv))):
             pltpu.make_async_copy(hbm.at[i], vm.at[i], in_sem.at[a, i]).wait()
         total = jnp.zeros((NBR_LEN, HEAD_DIM), jnp.float32)
-        for h in range(columns // HEAD_DIM):
-            cols = pl.ds(h * HEAD_DIM, HEAD_DIM)
-            weights = softmax(dot_t(nk[i, :, cols], nq[i, :, cols]) * softmax_scale, 0)
-            o = dot_first(weights, nv[i, :, cols]).astype(jnp.bfloat16)
-            own_out[h // group_heads, i, :, pl.ds((h % group_heads) * HEAD_DIM, HEAD_DIM)] = o
-            wide = o.astype(jnp.float32)
-            total = total + wide * wide
+        for base in range(0, columns // HEAD_DIM, 8):
+            together = range(base, base + 8)
+            cols = [pl.ds(h * HEAD_DIM, HEAD_DIM) for h in together]
+            scores = [dot_t(nk[i, :, c], nq[i, :, c]) * softmax_scale for c in cols]
+            weights = [softmax(x, 0) for x in scores]
+            outs = [dot_first(w, nv[i, :, c]).astype(jnp.bfloat16) for w, c in zip(weights, cols)]
+            for h, o in zip(together, outs):
+                own_out[h // group_heads, i, :, pl.ds((h % group_heads) * HEAD_DIM, HEAD_DIM)] = o
+                wide = o.astype(jnp.float32)
+                total = total + wide * wide
         stat1[pl.ds(i, 1), :] = jnp.sum(total.T, axis=0, keepdims=True)
         return carry
 
@@ -276,45 +279,49 @@
             out.append(copy)
         return out
 
-    def weigh_step(g, i):
-        keys = apart(kbufs[g][src_ref[i // NEIGHBOURS, i % NEIGHBOURS]])
-        scores = dot_t(keys, own_out[g, i]) * row_scale[pl.ds(i, 1), :]
-        weights = softmax(scores.reshape(group_heads, SEG_LEN, NBR_LEN), 1)
-        mixing[g, i] = weights.reshape(group_heads * SEG_LEN, NBR_LEN)
-
     def weigh(g):
         arrived(g)
 
-        def pair_step(t, carry):
-            for b in range(2):
-                weigh_step(g, 2 * t + b)
+        def some(t, carry):
+            rows = [4 * t + b for b in range(4)]
+            keys = [apart(kbufs[g][src_ref[i % NEIGHBOURS, i // NEIGHBOURS]]) for i in rows]
+            scores = [dot_t(k, own_out[g, i]) * row_scale[pl.ds(i, 1), :] for k, i in zip(keys, rows)]
+            weights = [softmax(x.reshape(group_heads, SEG_LEN, NBR_LEN), 1) for x in scores]
+            for i, w in zip(rows, weights):
+                mixing[g, i] = w.reshape(group_heads * SEG_LEN, NBR_LEN)
             return carry
 
-        lax.fori_loop(0, per_device // 2, pair_step, 0)
-
-    def cross_step(g, i):
-        values = apart(vbufs[g][src_ref[i // NEIGHBOURS, i % NEIGHBOURS]])
-        crossed = dot_first(mixing[g, i], values).astype(jnp.bfloat16)
-        both = (own_out[g, i].astype(jnp.float32) + crossed.astype(jnp.float32)).astype(jnp.bfloat16)
-        enc[g, NEIGHBOURS + i] = both
-        wide = both.astype(jnp.float32)
-        wide = wide * wide
-        total = wide[:, :HEAD_DIM]
-        for h in range(1, group_heads):
-            total = total + wide[:, h * HEAD_DIM:(h + 1) * HEAD_DIM]
-        if g > 0:
-            total = total + squares_acc[i]
-        if g < GROUPS - 1:
-            squares_acc[i] = total
-        else:
-            stat2[pl.ds(i, 1), :] = jnp.sum(total.T, axis=0, keepdims=True)
+        lax.fori_loop(0, per_device // 4, some, 0)
+
+    def cross_rows(g, rows):
+        values = [apart(vbufs[g][src_ref[i % NEIGHBOURS, i // NEIGHBOURS]]) for i in rows]
+        crossed = [dot_first(mixing[g, i], v).astype(jnp.bfloat16) for i, v in zip(rows, values)]
+        for i, x in zip(rows, crossed):
+            both = (own_out[g, i].astype(jnp.float32) + x.astype(jnp.float32)).astype(jnp.bfloat16)
+            enc[g, NEIGHBOURS + i] = both
+            wide = both.astype(jnp.float32)
+            wide = wide * wide
+            total = wide[:, :HEAD_DIM]
+            for h in range(1, group_heads):
+                total = total + wide[:, h * HEAD_DIM:(h + 1) * HEAD_DIM]
+            if g > 0:
+                total = total + squares_acc[i]
+            if g < GROUPS - 1:
+                squares_acc[i] = total
+            else:
+                stat2[pl.ds(i, 1), :] = jnp.sum(total.T, axis=0, keepdims=True)
 
     prior = []
+
+    def panel(g, u):
+        return enc[g, pl.ds(NEIGHBOURS * u, NEIGHBOURS)].reshape(NEIGHBOURS * NBR_LEN, width)
+
+    def ask(g, u):
+        asked[u, g] = dot_t(panel(g, u), apart(dq[u, :, pl.ds(g * width, width)]))
 
     def cross(g):
         arrived(GROUPS + g)
-        for i in range(per_device - NEIGHBOURS, per_device):
-            cross_step(g, i)
+        cross_rows(g, list(range(per_device - NEIGHBOURS, per_device)))
         copy = pltpu.make_async_remote_copy(
             src_ref=enc.at[g, pl.ds(per_device, NEIGHBOURS)], dst_ref=enc.at[g, pl.ds(0, NEIGHBOURS)],
             send_sem=prior_send.at[g], recv_sem=prior_recv.at[g],
@@ -323,11 +330,10 @@
         prior.append(copy)
 
         def rest_step(t, carry):
-            for b in range(2):
-                cross_step(g, 2 * t + b)
+            cross_rows(g, [3 * t + b for b in range(3)])
             return carry
 
-        lax.fori_loop(0, (per_device - NEIGHBOURS) // 2, rest_step, 0)
+        lax.fori_loop(0, (per_device - NEIGHBOURS) // 3, rest_step, 0)
 
     quarter = per_device // 4
     for j in range(4):
@@ -348,10 +354,14 @@
     for g in range(GROUPS):
         forward(g + 1)
         weigh(g)
+    dq_copy.wait()
     for g in range(GROUPS):
         if g + 1 < GROUPS:
             forward(GROUPS + 1 + g)
         cross(g)
+        if g + 1 < GROUPS:
+            for u in range(1, seg_dev):
+                ask(g, u)
 
     second_stats = exchange(1, stat2, peer2)
     behind_stats = []
@@ -363,7 +373,8 @@
             device_id={"span": after, "head": other}, device_id_type=MESH)
         copy.start()
         behind_stats.append(copy)
-    dq_copy.wait()
+    for u in range(1, seg_dev):
+        ask(GROUPS - 1, u)
     for copy in second_stats:
         copy.wait_recv()
     total2 = stat2[...]
@@ -375,10 +386,9 @@
         scale = jnp.concatenate([
             jnp.broadcast_to(key_scale[pl.ds(NEIGHBOURS * u + n, 1), :], (NBR_LEN, NBR_LEN)).T
             for n in range(NEIGHBOURS)], axis=0)
-        for g in range(GROUPS):
-            rows = enc[g, pl.ds(NEIGHBOURS * u, NEIGHBOURS)].reshape(NEIGHBOURS * NBR_LEN, width)
-            asked = apart(dq[u, :, pl.ds(g * width, width)])
-            out = dot_first(softmax(dot_t(rows, asked) * scale, 0), rows).astype(jnp.bfloat16)
+        weights = [softmax(asked[u, g] * scale, 0) for g in range(GROUPS)]
+        outs = [dot_first(w, panel(g, u)).astype(jnp.bfloat16) for g, w in enumerate(weights)]
+        for g, out in enumerate(outs):
             for h in range(group_heads):
                 lo = h * HEAD_DIM
                 out_ref[u, :, pl.ds(g * width + lo, HEAD_DIM)] = out[h * SEG_LEN:(h + 1) * SEG_LEN, lo:lo + HEAD_DIM]
@@ -399,6 +409,8 @@
     def _():
         enc[:, pl.ds(0, NEIGHBOURS)] = jnp.zeros((GROUPS, NEIGHBOURS, NBR_LEN, width), jnp.bfloat16)
 
+    for g in range(GROUPS):
+        ask(g, 0)
     decode_step(0, 0)
     for copy in list(sent.values()) + prior + first_stats + second_stats + behind_stats:
         copy.wait_send()
@@ -435,6 +447,7 @@
         + [
             pltpu.VMEM((GROUPS, per_device, NBR_LEN, width), bf16),
             pltpu.VMEM((GROUPS, per_device, width // HEAD_DIM * SEG_LEN, NBR_LEN), bf16),
+            pltpu.VMEM((SEG_DEV, GROUPS, NEIGHBOURS * NBR_LEN, width // HEAD_DIM * SEG_LEN), f32),
             pltpu.VMEM((GROUPS, per_device + NEIGHBOURS, NBR_LEN, width), bf16),
             pltpu.VMEM((per_device, NBR_LEN, HEAD_DIM), f32),
             pltpu.VMEM((per_device, NBR_LEN), f32),
@@ -447,8 +460,8 @@
             dma((3, per_device)),
             dma,
             dma((chunks,)),
-            dma((8, chunks)),
-            dma((8, chunks)),
+            dma((9, chunks)),
+            dma((9, chunks)),
             dma((3, heads_axis)),
             dma((3, heads_axis)),
             dma((GROUPS,)),
@@ -457,7 +470,7 @@
         compiler_params=pltpu.CompilerParams(
             collective_id=0, has_side_effects=True, vmem_limit_bytes=53 * 1024 * 1024),
     )(
-        sources,
+        sources.T,
         neighbour_query.reshape(neighbour_shape),
         neighbour_key.reshape(neighbour_shape),
         neighbour_value.reshape(neighbour_shape),

time: 57.3 us -> 53.3 us (0.930)
  Pallas kernels: 55.6 us -> 51.7 us
    pallas_call x1, Pallas kernels: 55.6 us -> 51.7 us  [fused_body(): pl.pallas_call(functools.partial(kernel, heads_axis, columns * heads_axis...]
    unnamed x2 -> x3, local copies, waits for them, and re-layouts: 1.56 us -> 1.47 us
where the time goes in v4:
time: 53.3 us; the launch traced here: 53.1 us
  Pallas kernels  51.7 us (97%)
  local copies, waits for them, and re-layouts  1.47 us (3%)
    pallas_call x1, Pallas kernels, fused_body(): pl.pallas_call(functools.partial(kernel, heads_axis, columns * heads_axis...  51.7 us
    unnamed x3, local copies, waits for them, and re-layouts  1.47 us

profile of v4, /device:TPU:0, one launch (start us, length us, event | category | flops | bytes accessed | tf_op | source)
XLA Modules:
  0.0 53.1 jit_solution(5066070001021190571)
XLA Ops:
  0.0 0.0 copy-start
  0.0 0.7 %copy-done = s32[4,2]{0,1:T(2,128)S(1)} copy-done((s32[4,2]{0,1:T(2,128)S(1)}, s32[4,2]{0,1:T(2,128)}, u32[]{:S(2)}) %copy-start) | copy-done | bytes 56
  0.7 51.7 %shard_map.73 = bf16[4,64,1024]{2,1,0:T(8,128)(2,1)S(1)} custom-call(s32[2,4]{1,0:T(2,128)S(1)} %bitcast.9, bf16[8,128,1024]{2,1,0:T(8,128)(2,1)} %bitcast.10, bf16[8,128,1024]{2,1,0:T(8,128)(2,1)} %bitcast.11, bf16[8,128,1024]{2,1,0:T(8,128)(2,1)} %bitcast.12, bf16[4,64,1024]{2,1,0:T(8,128)(2,1)} %bitcast.13, bf16[4,64,1024]{2,1,0:T(8,128)(2,1)} %bitcast.14, ...), custom_call_target="tpu_custom_call" | custom-call | tf_op jit(solution)/shard_map/pallas_call | solution.py:439
  52.3 0.8 %copy.9 = bf16[256,1024]{1,0:T(8,128)(2,1)} copy(bf16[256,1024]{1,0:T(8,128)(2,1)S(1)} %bitcast.8) | data formatting | bytes 1048576
Async XLA Ops:
  0.0 0.7 %copy-start = (s32[4,2]{0,1:T(2,128)S(1)}, s32[4,2]{0,1:T(2,128)}, u32[]{:S(2)}) copy-start(s32[4,2]{0,1:T(2,128)} %param.13) | copy-start | bytes 100

commit v5 on v4

--- a/solution.py
+++ b/solution.py
@@ -173,12 +173,6 @@
     before = lax.rem(me + span - 1, span)
     softmax_scale = HEAD_DIM ** (-0.5) / math.log(2.0)
 
-    for i in range(per_device):
-        for a, (hbm, vm) in enumerate(((nq_hbm, nq), (nk_hbm, nk), (nv_hbm, nv))):
-            pltpu.make_async_copy(hbm.at[i], vm.at[i], in_sem.at[a, i]).start()
-    dq_copy = pltpu.make_async_copy(dq_hbm, dq, dq_sem)
-    dq_copy.start()
-
     barrier = pltpu.get_barrier_semaphore()
     greeted = 0
     for target in (core, across, along):
@@ -188,11 +182,9 @@
         other = lax.rem(lane + k, heads_axis)
         pl.semaphore_signal(barrier, inc=1, device_id={"span": me, "head": other}, device_id_type=MESH)
         greeted += 1
-    for k in range(heads_axis):
-        other = lax.rem(lane + k, heads_axis)
-        for target in (after, before):
-            pl.semaphore_signal(barrier, inc=1, device_id={"span": target, "head": other}, device_id_type=MESH)
-            greeted += 1
+    for target in (after, before):
+        pl.semaphore_signal(barrier, inc=1, device_id={"span": target, "head": lane}, device_id_type=MESH)
+        greeted += 1
     pl.semaphore_wait(barrier, greeted)
 
     chunks = 2 * GROUPS
@@ -227,6 +219,14 @@
     local = []
     for j in range(chunks):
         direct(j)
+
+    for i in range(per_device):
+        for a, (hbm, vm) in enumerate(((nq_hbm, nq), (nk_hbm, nk), (nv_hbm, nv))):
+            pltpu.make_async_copy(hbm.at[i], vm.at[i], in_sem.at[a, i]).start()
+    dq_copy = pltpu.make_async_copy(dq_hbm, dq, dq_sem)
+    dq_copy.start()
+
+    for j in range(chunks):
         push(4, j, source(j), block(j, me), core)
         copy = pltpu.make_async_copy(source(j), block(j, me), local_sem.at[j])
         copy.start()
@@ -364,17 +364,23 @@
                 ask(g, u)
 
     second_stats = exchange(1, stat2, peer2)
+    handed = pltpu.make_async_remote_copy(
+        src_ref=stat2, dst_ref=behind2.at[0],
+        send_sem=stat_send.at[2, 0], recv_sem=stat_recv.at[2, 0],
+        device_id={"span": after, "head": lane}, device_id_type=MESH)
+    handed.start()
+    for u in range(1, seg_dev):
+        ask(GROUPS - 1, u)
+    handed.wait_recv()
     behind_stats = []
-    for k in range(heads_axis):
+    for k in range(1, heads_axis):
         other = lax.rem(lane + k, heads_axis)
         copy = pltpu.make_async_remote_copy(
-            src_ref=stat2, dst_ref=behind2.at[k],
+            src_ref=behind2.at[0], dst_ref=behind2.at[k],
             send_sem=stat_send.at[2, k], recv_sem=stat_recv.at[2, k],
-            device_id={"span": after, "head": other}, device_id_type=MESH)
+            device_id={"span": me, "head": other}, device_id_type=MESH)
         copy.start()
         behind_stats.append(copy)
-    for u in range(1, seg_dev):
-        ask(GROUPS - 1, u)
     for copy in second_stats:
         copy.wait_recv()
     total2 = stat2[...]
@@ -412,7 +418,7 @@
     for g in range(GROUPS):
         ask(g, 0)
     decode_step(0, 0)
-    for copy in list(sent.values()) + prior + first_stats + second_stats + behind_stats:
+    for copy in [handed] + list(sent.values()) + prior + first_stats + second_stats + behind_stats:
         copy.wait_send()
 
 

time: 53.3 us -> 55.4 us (1.039)
  Pallas kernels: 51.7 us -> 53.7 us
    pallas_call x1, Pallas kernels: 51.7 us -> 53.7 us  [fused_body(): pl.pallas_call(functools.partial(kernel, heads_axis, columns * heads_axis...]
where the time goes in v5:
time: 55.4 us; the launch traced here: 55.2 us
  Pallas kernels  53.7 us (97%)
  local copies, waits for them, and re-layouts  1.47 us (3%)
    pallas_call x1, Pallas kernels, fused_body(): pl.pallas_call(functools.partial(kernel, heads_axis, columns * heads_axis...  53.7 us
    unnamed x3, local copies, waits for them, and re-layouts  1.47 us

profile of v5, /device:TPU:0, one launch (start us, length us, event | category | flops | bytes accessed | tf_op | source)
XLA Modules:
  0.0 55.2 jit_solution(13234465593204238511)
XLA Ops:
  0.0 0.0 copy-start
  0.0 0.7 %copy-done = s32[4,2]{0,1:T(2,128)S(1)} copy-done((s32[4,2]{0,1:T(2,128)S(1)}, s32[4,2]{0,1:T(2,128)}, u32[]{:S(2)}) %copy-start) | copy-done | bytes 56
  0.7 53.7 %shard_map.73 = bf16[4,64,1024]{2,1,0:T(8,128)(2,1)S(1)} custom-call(s32[2,4]{1,0:T(2,128)S(1)} %bitcast.9, bf16[8,128,1024]{2,1,0:T(8,128)(2,1)} %bitcast.10, bf16[8,128,1024]{2,1,0:T(8,128)(2,1)} %bitcast.11, bf16[8,128,1024]{2,1,0:T(8,128)(2,1)} %bitcast.12, bf16[4,64,1024]{2,1,0:T(8,128)(2,1)} %bitcast.13, bf16[4,64,1024]{2,1,0:T(8,128)(2,1)} %bitcast.14, ...), custom_call_target="tpu_custom_call" | custom-call | tf_op jit(solution)/shard_map/pallas_call | solution.py:445
  54.4 0.8 %copy.9 = bf16[256,1024]{1,0:T(8,128)(2,1)} copy(bf16[256,1024]{1,0:T(8,128)(2,1)S(1)} %bitcast.8) | data formatting | bytes 1048576
Async XLA Ops:
  0.0 0.7 %copy-start = (s32[4,2]{0,1:T(2,128)S(1)}, s32[4,2]{0,1:T(2,128)}, u32[]{:S(2)}) copy-start(s32[4,2]{0,1:T(2,128)} %param.13) | copy-start | bytes 100

commit v6 on v4

--- a/solution.py
+++ b/solution.py
@@ -173,12 +173,6 @@
     before = lax.rem(me + span - 1, span)
     softmax_scale = HEAD_DIM ** (-0.5) / math.log(2.0)
 
-    for i in range(per_device):
-        for a, (hbm, vm) in enumerate(((nq_hbm, nq), (nk_hbm, nk), (nv_hbm, nv))):
-            pltpu.make_async_copy(hbm.at[i], vm.at[i], in_sem.at[a, i]).start()
-    dq_copy = pltpu.make_async_copy(dq_hbm, dq, dq_sem)
-    dq_copy.start()
-
     barrier = pltpu.get_barrier_semaphore()
     greeted = 0
     for target in (core, across, along):
@@ -227,6 +221,14 @@
     local = []
     for j in range(chunks):
         direct(j)
+
+    for i in range(per_device):
+        for a, (hbm, vm) in enumerate(((nq_hbm, nq), (nk_hbm, nk), (nv_hbm, nv))):
+            pltpu.make_async_copy(hbm.at[i], vm.at[i], in_sem.at[a, i]).start()
+    dq_copy = pltpu.make_async_copy(dq_hbm, dq, dq_sem)
+    dq_copy.start()
+
+    for j in range(chunks):
         push(4, j, source(j), block(j, me), core)
         copy = pltpu.make_async_copy(source(j), block(j, me), local_sem.at[j])
         copy.start()

time: 53.3 us -> 53.3 us (level)
  no operation moved by 1% of the time
where the time goes in v6:
time: 53.3 us; the launch traced here: 53.1 us
  Pallas kernels  51.6 us (97%)
  local copies, waits for them, and re-layouts  1.47 us (3%)
    pallas_call x1, Pallas kernels, fused_body(): pl.pallas_call(functools.partial(kernel, heads_axis, columns * heads_axis...  51.6 us
    unnamed x3, local copies, waits for them, and re-layouts  1.47 us

profile of v6, /device:TPU:0, one launch (start us, length us, event | category | flops | bytes accessed | tf_op | source)
XLA Modules:
  0.0 53.1 jit_solution(6453264948027058361)
XLA Ops:
  0.0 0.0 copy-start
  0.0 0.7 %copy-done = s32[4,2]{0,1:T(2,128)S(1)} copy-done((s32[4,2]{0,1:T(2,128)S(1)}, s32[4,2]{0,1:T(2,128)}, u32[]{:S(2)}) %copy-start) | copy-done | bytes 56
  0.7 51.6 %shard_map.73 = bf16[4,64,1024]{2,1,0:T(8,128)(2,1)S(1)} custom-call(s32[2,4]{1,0:T(2,128)S(1)} %bitcast.9, bf16[8,128,1024]{2,1,0:T(8,128)(2,1)} %bitcast.10, bf16[8,128,1024]{2,1,0:T(8,128)(2,1)} %bitcast.11, bf16[8,128,1024]{2,1,0:T(8,128)(2,1)} %bitcast.12, bf16[4,64,1024]{2,1,0:T(8,128)(2,1)} %bitcast.13, bf16[4,64,1024]{2,1,0:T(8,128)(2,1)} %bitcast.14, ...), custom_call_target="tpu_custom_call" | custom-call | tf_op jit(solution)/shard_map/pallas_call | solution.py:441
  52.3 0.8 %copy.9 = bf16[256,1024]{1,0:T(8,128)(2,1)} copy(bf16[256,1024]{1,0:T(8,128)(2,1)S(1)} %bitcast.8) | data formatting | bytes 1048576
Async XLA Ops:
  0.0 0.7 %copy-start = (s32[4,2]{0,1:T(2,128)S(1)}, s32[4,2]{0,1:T(2,128)}, u32[]{:S(2)}) copy-start(s32[4,2]{0,1:T(2,128)} %param.13) | copy-start | bytes 100
